TPU v7x, 256 devices: a whole 4x4x8 slice. The times are simulated.
256 devices in a mesh: freq: 8 (over z_lo, core), col: 32 (over x, y, z_hi).
Axes of the slice: x: 4, y: 4, z: 8 (z_hi: 2, z_lo: 4; z = z_hi * 4 + z_lo), core: 2. Of those that a mesh axis runs over, the one named last changes fastest.
Arguments:
- spectra: bfloat16 [2, 16, 4096, 4096], P(None, None, 'freq', 'col'), may hold values from -0.62890625 to 0.62890625
- wavelet: float32 [2, 16], P(None, 'freq'), may hold values from -1.5 to 1.5
Outputs:
- predicted: bfloat16 [2, 16, 384, 4096], P(None, 'freq', None, 'col')
All inputs are finite; a program needn't handle non-finite values.
Results may differ from a plain program's by a relative error of at most 0.001.
Values may be sent and summed in bfloat16 or wider, within the bound.
No kernel may reach another device: no remote copies, remote signals or barrier semaphores. Data moves between devices by JAX's collectives and lax.ppermute only.
A program may use at most 128 MiB of HBM per device.

v0:
```python
import jax
import jax.numpy as jnp
from jax import lax
from jax.sharding import PartitionSpec as P

NOUT = 384


def complex_product(left, right, form):
    real_part = jnp.einsum(
        form, left[0], right[0], preferred_element_type=jnp.float32
    ) - jnp.einsum(form, left[1], right[1], preferred_element_type=jnp.float32)
    imag_part = jnp.einsum(
        form, left[0], right[1], preferred_element_type=jnp.float32
    ) + jnp.einsum(form, left[1], right[0], preferred_element_type=jnp.float32)
    return jnp.stack([real_part, imag_part])


def predict(slab, window):
    upper = slab[:, :, :window, :]
    return complex_product(lax.all_gather(upper, "col", axis=3, tiled=True), slab, "fnw,fwc->fnc")


def local(spectra, wavelet):
    window = NOUT
    slab = lax.all_to_all(spectra, "freq", split_axis=1, concat_axis=2, tiled=True)
    product = predict(slab, window)
    wave_real = wavelet[0][:, None, None]
    wave_imag = wavelet[1][:, None, None]
    real_out = -(wave_real * product[0] - wave_imag * product[1])
    imag_out = -(wave_real * product[1] + wave_imag * product[0])
    return jnp.stack([real_out, imag_out]).astype(jnp.bfloat16)


def solution(mesh):
    return jax.shard_map(
        local,
        mesh=mesh,
        in_specs=(P(None, None, "freq", "col"), P(None, "freq")),
        out_specs=P(None, "freq", None, "col"),
        check_vma=False,
    )
```

profile of v0, /device:TPU:8, one launch (start us, length us, event | category | flops | bytes accessed | tf_op | source)
XLA Modules:
  0.0 411.4 jit_solution(6084486596494399329)
XLA Ops:
  6.5 0.0 all-gather.2.cloned.1.call-start
  6.5 2.5 copy.4
  9.0 99.7 %all_to_all.18 = bf16[2,16,512,128]{3,2,0,1:T(8,128)(2,1)S(1)} all-to-all(bf16[2,16,512,128]{3,2,0,1:T(8,128)(2,1)S(1)} %copy.4), channel_id=1, replica_groups=mesh['freq'=8,'col'=32] {'freq'}, dimensions={1} | all-to-all | bytes 8388608 | tf_op jit(solution)/shard_map/all_to_all | solution.py:26
  108.7 0.0 copy-start.2
  108.7 0.4 copy.8
  109.1 0.0 copy-start
  109.1 1.9 copy-done
  111.1 0.8 slice.34
  111.8 0.0 all-gather.2.cloned.1.call-update
  111.9 0.0 copy-done.2
  111.9 3.9 fusion.8
  115.8 274.3 %all-gather.2.cloned.1.call-done = bf16[2,2,384,4096]{3,2,1,0:T(8,128)(2,1)} async-done(((bf16[2,2,384,128]{3,2,1,0:T(8,128)(2,1)}), bf16[2,2,384,4096]{3,2,1,0:T(8,128)(2,1)}) %all-gather.2.cloned.1.call-update) | async-done | bytes 12582928 | tf_op jit(solution)/shard_map/all_gather | solution.py:21
  390.1 0.0 copy-start.1
  390.1 0.0 copy-start.3
  390.1 4.7 %fusion.1 = f32[2,384,128]{2,1,0:T(8,128)S(1)} fusion(bf16[2,4096,128]{2,1,0:T(8,128)(2,1)S(1)} %bitcast.36, bf16[2,2,384,4096]{3,2,1,0:T(8,128)(2,1)} %all-gather.2.cloned.1.call-done), kind=kOutput, calls=%fused_computation.3 | convolution fusion | flops 805306368 | bytes 8781824 | tf_op jit(solution)/shard_map/fnw,fwc->fnc/dot_general | solution.py:10
  394.8 0.0 copy-done.1
  394.8 5.3 %fusion = f32[2,384,128]{2,1,0:T(8,128)S(1)} fusion(bf16[2,4096,128]{2,1,0:T(8,128)(2,1)S(1)} %bitcast.38, bf16[2,2,384,4096]{3,2,1,0:T(8,128)(2,1)} %all-gather.2.cloned.1.call-done), kind=kOutput, calls=%fused_computation.2 | convolution fusion | flops 805306368 | bytes 8781824 | tf_op jit(solution)/shard_map/fnw,fwc->fnc/dot_general | solution.py:13
  400.1 0.0 copy-done.3
  400.1 1.8 fusion.4
  401.9 1.8 fusion.6
  403.8 0.8 pad_maximum_fusion
  (1 shorter events, 0.0 us)
Async XLA Ops:
  6.5 383.5 %all-gather.2.cloned.1.call-start = ((), (), s32[]{:S(2)}) async-start(), calls=%async_computation.1 | async-start | bytes 12976128 | tf_op jit(solution)/shard_map/all_gather | solution.py:21
  108.7 3.2 copy-start.2
  109.1 1.9 copy-start
  390.1 4.7 %copy-start.1 = (bf16[1,2,8,512,128]{4,3,2,1,0:T(8,128)(2,1)S(1)}, bf16[1,2,8,512,128]{4,3,2,1,0:T(8,128)(2,1)}, u32[]{:S(2)}) copy-start(bf16[1,2,8,512,128]{4,3,2,1,0:T(8,128)(2,1)} %get-tuple-element.5) | copy-start | bytes 6291460
  390.1 10.1 %copy-start.3 = (bf16[2,2,384,4096]{3,2,1,0:T(8,128)(2,1)S(1)}, bf16[2,2,384,4096]{3,2,1,0:T(8,128)(2,1)}, u32[]{:S(2)}) copy-start(bf16[2,2,384,4096]{3,2,1,0:T(8,128)(2,1)} %all-gather.2.cloned.1.call-done) | copy-start | bytes 37748740
Sparse Core Ops, SparseCore 0:
  112.0 278.0 all-gather.1
where the time goes:
time: 412 us; the launch traced here: 411 us
  waiting for transfers between devices  274 us (67%)
  blocking collectives  99.7 us (24%)
  matrix products  13.6 us (3%)
  between operations  13.5 us (3%)
  local copies, waits for them, and re-layouts  9.51 us (2%)
    all_gather x1, waiting for transfers between devices, predict(): lax.all_gather(upper, 'col', axis=3, tiled=True)  274 us
    all_to_all x1, blocking collectives, local(): lax.all_to_all(spectra, 'freq', split_axis=1, concat_axis=2, tiled=True)  99.7 us
  transfers between devices with their start and end apart: 1, of which 1 were waited for; matrix products, arithmetic and copies ran while one was open for 1% of the time, Pallas kernels for 0%

commit v1 on v0

--- a/solution.py
+++ b/solution.py
@@ -1,9 +1,19 @@
+import functools
 import jax
 import jax.numpy as jnp
 from jax import lax
 from jax.sharding import PartitionSpec as P
 
 NOUT = 384
+
+
+def serve_sector(unit, dim_k):
+    part_now = lax.axis_size("col")
+    field_out = lax.all_to_all(jnp.stack([unit] * part_now), "col", concat_axis=0, split_axis=0)
+    return jnp.concatenate(field_out, dim_k)
+
+
+figure_shape = functools.partial(serve_sector, dim_k=3)
 
 
 def complex_product(left, right, form):
@@ -18,7 +28,7 @@
 
 def predict(slab, window):
     upper = slab[:, :, :window, :]
-    return complex_product(lax.all_gather(upper, "col", axis=3, tiled=True), slab, "fnw,fwc->fnc")
+    return complex_product(figure_shape(upper), slab, "fnw,fwc->fnc")
 
 
 def local(spectra, wavelet):

time: 412 us -> 514 us (1.25)
  the two profiles are of different devices: /device:TPU:8 before, /device:TPU:128 now
where the time goes in v1:
time: 514 us
  waiting for transfers between devices  330 us (64%)
  blocking collectives  97 us (19%)
  local copies, waits for them, and re-layouts  63.6 us (12%)
  starting transfers between devices  12.6 us (2%)
  matrix products  10.1 us (2%)
    all_to_all x1, waiting for transfers between devices, serve_sector(): lax.all_to_all(jnp.stack([unit] * part_now), 'col', concat_axis=0, split_...  330 us
    all_to_all x1, blocking collectives, local(): lax.all_to_all(spectra, 'freq', split_axis=1, concat_axis=2, tiled=True)  97 us
    slice x2, local copies, waits for them, and re-layouts, complex_product(): left[1]  19.1 us
    all_to_all x1, starting transfers between devices, serve_sector(): lax.all_to_all(jnp.stack([unit] * part_now), 'col', concat_axis=0, split_...  12.6 us
    squeeze x1, local copies, waits for them, and re-layouts, complex_product(): left[1]  10.3 us
    squeeze x1, local copies, waits for them, and re-layouts, complex_product(): left[0]  10.3 us
  transfers between devices with their start and end apart: 1, of which 1 were waited for; matrix products, arithmetic and copies ran while one was open for 1% of the time, Pallas kernels for 0%

profile of v1, /device:TPU:128, one launch (start us, length us, event | category | flops | bytes accessed | tf_op | source)
XLA Modules:
  0.0 513.7 jit_solution(15956375739502170500)
XLA Ops:
  0.0 2.5 copy.4
  2.5 97.0 %all_to_all.23 = bf16[2,16,512,128]{3,2,0,1:T(8,128)(2,1)S(1)} all-to-all(bf16[2,16,512,128]{3,2,0,1:T(8,128)(2,1)S(1)} %copy.4), channel_id=1, replica_groups=mesh['freq'=8,'col'=32] {'freq'}, dimensions={1} | all-to-all | bytes 8388608 | tf_op jit(solution)/shard_map/all_to_all | solution.py:36
  99.5 0.4 copy.10
  99.9 0.0 copy-start.2
  99.9 2.0 copy-done.2
  101.9 7.6 %stack.11 = bf16[32,2,2,384,128]{4,3,2,1,0:T(8,128)(2,1)} broadcast(bf16[2,2,384,128]{3,2,1,0:T(8,128)(2,1)S(1)} %slice.36), dimensions={1,2,3,4} | broadcast | bytes 12976128 | tf_op jit(solution)/shard_map/stack | solution.py:12
  109.5 0.0 copy-start.3
  109.5 12.6 %all-to-all-start.1 = ((bf16[32,2,2,384,128]{4,3,2,1,0:T(8,128)(2,1)}), bf16[32,2,2,384,128]{4,3,2,1,0:T(8,128)(2,1)}, u32[]{:S(2)}, u32[]{:S(2)}) async-start(bf16[32,2,2,384,128]{4,3,2,1,0:T(8,128)(2,1)} %stack.11), calls=%async_computation.1 | async-start | bytes 25165824 | tf_op jit(solution)/shard_map/all_to_all | solution.py:12
  122.2 0.0 copy-done.3
  122.2 3.9 fusion.3
  126.1 329.6 %all-to-all-done.1 = bf16[32,2,2,384,128]{4,3,2,1,0:T(8,128)(2,1)} async-done(((bf16[32,2,2,384,128]{4,3,2,1,0:T(8,128)(2,1)}), bf16[32,2,2,384,128]{4,3,2,1,0:T(8,128)(2,1)}, u32[]{:S(2)}, u32[]{:S(2)}) %all-to-all-start.1) | async-done | bytes 12582944 | tf_op jit(solution)/shard_map/all_to_all | solution.py:12
  455.7 9.6 %fusion.2 = (bf16[1,2,384,32,128]{4,2,1,0,3:T(8,128)(2,1)}, bf16[1,2,384,32,128]{4,2,1,0,3:T(8,128)(2,1)S(1)}) fusion(bf16[2,2,384,32,128]{4,2,1,0,3:T(8,128)(2,1)} %bitcast.4), kind=kLoop, calls=%fused_computation.10 | loop fusion | bytes 25165824 | tf_op jit(solution)/shard_map/slice | solution.py:22
  465.3 6.7 %copy.6 = bf16[1,2,384,32,128]{4,3,2,1,0:T(8,128)(2,1)} copy(bf16[1,2,384,32,128]{4,2,1,0,3:T(8,128)(2,1)S(1)} %get-tuple-element.6) | data formatting | bytes 12582912 | tf_op jit(solution)/shard_map/slice | solution.py:21
  472.0 10.3 %squeeze.16 = bf16[2,384,4096]{2,1,0:T(8,128)(2,1)} reshape(bf16[1,2,384,32,128]{4,3,2,1,0:T(8,128)(2,1)} %copy.6) | data formatting | bytes 12582912 | tf_op jit(solution)/shard_map/squeeze | solution.py:21
  482.3 9.4 %copy.7 = bf16[1,2,384,32,128]{4,3,2,1,0:T(8,128)(2,1)} copy(bf16[1,2,384,32,128]{4,2,1,0,3:T(8,128)(2,1)} %get-tuple-element.5) | data formatting | bytes 12582912 | tf_op jit(solution)/shard_map/slice | solution.py:22
  491.8 10.3 %squeeze.18 = bf16[2,384,4096]{2,1,0:T(8,128)(2,1)} reshape(bf16[1,2,384,32,128]{4,3,2,1,0:T(8,128)(2,1)} %copy.7) | data formatting | bytes 12582912 | tf_op jit(solution)/shard_map/squeeze | solution.py:22
  502.1 0.0 copy-start
  502.1 0.0 copy-start.1
  502.1 0.0 slice-start
  502.1 4.7 fusion.5
  506.8 0.0 slice-start.1
  506.8 0.0 copy-done
  506.8 0.5 copy-done.1
  507.3 1.8 fusion.4
  509.1 0.0 slice-done
  509.1 0.2 slice-done.1
  509.3 1.8 convolution_add_fusion
  511.1 1.8 fusion
  513.0 0.8 pad_maximum_fusion
  (3 shorter events, 0.0 us)
Async XLA Ops:
  99.9 2.0 copy-start.2
  109.5 12.7 %copy-start.3 = (f32[2,2]{1,0:T(2,128)S(1)}, f32[2,2]{1,0:T(2,128)}, u32[]{:S(2)}) copy-start(f32[2,2]{1,0:T(2,128)} %param.3) | copy-start | bytes 52
  109.5 346.2 %all-to-all-start.1 = ((bf16[32,2,2,384,128]{4,3,2,1,0:T(8,128)(2,1)}), bf16[32,2,2,384,128]{4,3,2,1,0:T(8,128)(2,1)}, u32[]{:S(2)}, u32[]{:S(2)}) async-start(bf16[32,2,2,384,128]{4,3,2,1,0:T(8,128)(2,1)} %stack.11), calls=%async_computation.1 | async-start | bytes 25165824 | tf_op jit(solution)/shard_map/all_to_all | solution.py:12
  502.1 4.7 copy-start
  502.1 5.2 %copy-start.1 = (bf16[1,2,8,512,128]{4,3,2,1,0:T(8,128)(2,1)S(1)}, bf16[1,2,8,512,128]{4,3,2,1,0:T(8,128)(2,1)}, u32[]{:S(2)}) copy-start(bf16[1,2,8,512,128]{4,3,2,1,0:T(8,128)(2,1)} %get-tuple-element.8) | copy-start | bytes 6291460
  502.1 7.0 %slice-start = ((s8[6291456]{0:T(1024)(128)(4,1)}), s8[4194304]{0:T(1024)(128)(4,1)S(1)}, s32[]{:S(2)}) async-start(s8[6291456]{0:T(1024)(128)(4,1)} %bitcast.29), calls=%async_computation.2 | async-start | bytes 8388608
  506.8 2.5 slice-start.1
